TPU v7x, 32 devices: a whole 2x2x4 slice. The times are simulated.
32 devices in a mesh: groups: 2 (over y), chan: 8 (over z, x), tm: 2 (over core).
Axes of the slice: x: 2, y: 2, z: 4, core: 2. Of those that a mesh axis runs over, the one named last changes fastest.
Arguments:
- record: bfloat16 [8, 4096, 1000], P('tm', ('groups', 'chan')), parts along dimension 1
- flags: int32 [4096], P(('groups', 'chan')), parts along dimension 0, may hold values 0 or 1
- plan: int32 [4], replicated, may hold values from 1 to 7, as said below
Outputs:
- stacked: bfloat16 [4, 4, 4096, 256], P('tm', None, ('groups', 'chan')), parts along dimension 2
There are 2 independent parts, one for each index of `groups`. A program takes and returns all parts, laid end to end along the dimension named above; an argument that names none is the same for every part. Nothing has to cross between parts.
Inputs may be any that keep to these rules, and one draw needn't show every extreme that they name: `plan`: 4 distinct offsets; one of them equals 7.
All inputs are finite; a program needn't handle non-finite values. No bound on the sum of `flags` on one device may be relied on, other than what follows from the above.
Results may differ from a plain program's by a relative error of at most 0.0082.
Values may be sent and summed in bfloat16 or wider, within the bound.
No kernel may reach another device: no remote copies, remote signals or barrier semaphores. Data moves between devices by JAX's collectives and lax.ppermute only.
A program may use at most 64 MiB of HBM per device.

v0:
```python
from functools import partial
import math

import numpy as np

import jax
import jax.numpy as jnp
from jax import lax
from jax.experimental import pallas as pl
from jax.experimental.pallas import tpu as pltpu
from jax.sharding import PartitionSpec as P


NFREQ = 32
FLO = 5
LAGS = 4
LAGSTEP = 3
ROUNDS = 4

TWO_PI = 2.0 * math.pi
VMEM = pltpu.MemorySpace.VMEM
SMEM = pltpu.MemorySpace.SMEM
HBM = pltpu.MemorySpace.HBM
BF16 = jnp.bfloat16
F32 = jnp.float32


def padded(samples):
    return -(-samples // 256) * 256


def basis_table(samples):
    phase = (FLO + np.arange(NFREQ))[:, None] * np.arange(samples)[None, :] % samples
    angle = phase.astype(np.float32) * np.float32(TWO_PI / samples)
    rows = np.concatenate([np.cos(angle), -np.sin(angle)], 0).astype(jnp.bfloat16)
    table = np.zeros((2 * NFREQ + 16, padded(samples)), jnp.bfloat16)
    table[: 2 * NFREQ, :samples] = rows
    table[2 * NFREQ, :samples] = 1
    sums = rows.astype(np.float64).sum(1).astype(np.float32)
    return table, np.repeat(sums[:, None], 128, 1)


def turn_table(samples):
    ticks = (np.arange(LAGS) - LAGS // 2) * LAGSTEP
    phase = (FLO + np.arange(NFREQ))[None, :] * ticks[:, None] % samples
    angle = phase.astype(np.float32) * np.float32(TWO_PI / samples)
    table = np.stack([np.cos(angle), np.sin(angle)], 1).astype(np.float32)
    return np.repeat(table[..., None], 128, 3)


def rest_mask(n_chan, plan):
    mask = jnp.int32(0)
    for o in range(3, n_chan - 1):
        for r in range(ROUNDS):
            mask += (plan[r] == o).astype(jnp.int32) << (o - 3)
    return mask


def place_of(offset, plan):
    place = jnp.int32(ROUNDS)
    for r in range(ROUNDS):
        place = jnp.where(plan[r] == offset, r, place)
    return place


def spectra_kernel(flags_hbm, basis_hbm, sums_hbm, record_hbm, spec_ref, held, basis, sums_held, flags, sems):
    windows, samples, width = record_hbm.shape
    copies = [
        pltpu.make_async_copy(record_hbm.at[w], held.at[w, pl.ds(0, samples)], sems.at[w]) for w in range(windows)
    ]
    small = [(basis_hbm, basis), (flags_hbm, flags), (sums_hbm, sums_held)]
    small = [pltpu.make_async_copy(src, dst, sems.at[windows + i]) for i, (src, dst) in enumerate(small)]
    copies[0].start()
    for copy in small + copies[1:]:
        copy.start()
    pad = held.shape[1] - samples
    for w in range(windows):
        held[w, samples:, :] = jnp.zeros((pad, width), BF16)
    for copy in small:
        copy.wait()
    good = flags[...].astype(F32) * (1.0 / math.sqrt(samples))
    sums = jnp.concatenate([sums_held[...]] * (width // 128), axis=1)
    rows = 2 * NFREQ
    for w in range(windows):
        copies[w].wait()
        out = jnp.dot(basis[...], held[w], preferred_element_type=F32)
        mean = out[rows : rows + 1] * (1.0 / samples)
        centred = held[w, :samples, :].astype(F32) - mean
        power = jnp.sum(centred * centred, axis=0, keepdims=True) * (1.0 / samples)
        scale = good / jnp.sqrt(power + 1e-05)
        spec_ref[w * rows : (w + 1) * rows, :] = ((out[:rows] - sums * mean) * scale).astype(BF16)


def turn_kernel(n_chan, plan_ref, mine_ref, other_ref, table_ref, turned_ref, mask_ref):
    mask_ref[0] = rest_mask(n_chan, [plan_ref[r] for r in range(ROUNDS)]) if few_sets(n_chan) else jnp.int32(0)
    lags = turned_ref.shape[0]
    first = lax.axis_index("tm") * lags
    depth, width = mine_ref.shape
    for half, ref in enumerate((mine_ref, other_ref)):
        for lag in range(lags):
            cosine = jnp.concatenate([table_ref[first + lag, 0]] * (width // 128), axis=1)
            sine = jnp.concatenate([table_ref[first + lag, 1]] * (width // 128), axis=1)
            parts = []
            for w in range(depth // (2 * NFREQ)):
                start = w * 2 * NFREQ
                real = ref[start : start + NFREQ, :].astype(F32)
                imag = ref[start + NFREQ : start + 2 * NFREQ, :].astype(F32)
                parts += [real * cosine + imag * sine, imag * cosine - real * sine]
            turned = jnp.concatenate(parts, axis=0).T.astype(BF16)
            turned_ref[lag, :, half * depth : (half + 1) * depth] = turned


def correlate_kernel(scale, labels, plan_ref, turned_ref, *refs):
    blocks = len(labels)
    mine, other, (out_ref, held, sems) = refs[:blocks], refs[blocks : 2 * blocks], refs[-3:]
    lags, _, depth = turned_ref.shape
    half = depth // 2
    plan = [plan_ref[r] for r in range(ROUNDS)]
    places = []
    for s, label in enumerate(labels):
        if isinstance(label, tuple):
            label = jnp.where(lax.axis_index("tm") == 0, *label)
        places.append(jnp.int32(s) if label is None else place_of(label, plan))

    def copy(s, lag):
        return pltpu.make_async_copy(held.at[s, lag], out_ref.at[lag, places[s]], sems.at[s, lag])

    for s in range(blocks):

        @pl.when(places[s] < ROUNDS)
        def _():
            for lag in range(lags):
                total = jnp.dot(turned_ref[lag, :, :half], mine[s][...], preferred_element_type=F32)
                total += jnp.dot(turned_ref[lag, :, half:], other[s][...], preferred_element_type=F32)
                held[s, lag] = (total * scale).astype(BF16)
                copy(s, lag).start()

    for s in range(blocks):

        @pl.when(places[s] < ROUNDS)
        def _():
            for lag in range(lags):
                copy(s, lag).wait()


def correlate(plan, turned, pairs, labels, out=None):
    lags, width, depth = turned.shape
    blocks = len(pairs)
    scale = 1.0 / math.sqrt(depth // 2)
    given = [plan, turned] + [p[0] for p in pairs] + [p[1] for p in pairs]
    specs = [pl.BlockSpec(memory_space=SMEM)] + [pl.BlockSpec(memory_space=VMEM)] * (1 + 2 * blocks)
    if out is not None:
        given.append(out)
        specs.append(pl.BlockSpec(memory_space=HBM))
    return pl.pallas_call(
        partial(correlate_kernel, scale, labels),
        out_shape=HBM((lags, ROUNDS, width, width), BF16),
        in_specs=specs,
        out_specs=pl.BlockSpec(memory_space=HBM),
        scratch_shapes=[
            pltpu.VMEM((blocks, lags, width, width), BF16),
            pltpu.SemaphoreType.DMA((blocks, lags)),
        ],
        input_output_aliases={} if out is None else {len(given) - 1: 0},
        compiler_params=pltpu.CompilerParams(vmem_limit_bytes=KERNEL_VMEM),
        cost_estimate=pl.CostEstimate(flops=blocks << 28, bytes_accessed=blocks << 20, transcendentals=0),
        name="correlate",
    )(*given)


def turn(spec, samples, plan):
    depth, width = spec.shape
    other = swap(spec)
    return pl.pallas_call(
        partial(turn_kernel, lax.axis_size("chan")),
        out_shape=(
            jax.ShapeDtypeStruct((LAGS // 2, width, 2 * depth), BF16),
            jax.ShapeDtypeStruct((1,), jnp.int32),
        ),
        in_specs=[pl.BlockSpec(memory_space=SMEM)] + [pl.BlockSpec(memory_space=VMEM)] * 3,
        out_specs=(pl.BlockSpec(memory_space=VMEM), pl.BlockSpec(memory_space=SMEM)),
        compiler_params=pltpu.CompilerParams(vmem_limit_bytes=KERNEL_VMEM),
        cost_estimate=pl.CostEstimate(flops=4 << 20, bytes_accessed=4 << 20, transcendentals=0),
        name="turn",
    )(plan, spec, other, jnp.asarray(turn_table(samples)))


KERNEL_VMEM = 8 << 20


def few_sets(n_chan):
    return n_chan == 2 * ROUNDS


def hop(value, offset):
    pairs = [(source, source ^ offset) for source in range(lax.axis_size("chan"))]
    return lax.ppermute(value, "chan", pairs)


def swap(value):
    return lax.ppermute(value, "tm", [(0, 1), (1, 0)])


def with_swap(block):
    return block, swap(block)


def split_hop(first, second, hops):
    n_chan = lax.axis_size("chan")
    value = first if first is second else jnp.where(lax.axis_index("tm") == 0, first, second)
    pairs = [(2 * c + t, 2 * (c ^ hops[t]) + t) for c in range(n_chan) for t in range(2)]
    return lax.ppermute(value, ("chan", "tm"), pairs)


def correlate_rest(mask, crossed, near, turned, plan, out):
    top = lax.axis_size("chan") - 1
    here = {1: near[0], 2: near[1], top: crossed}
    wanted = [o + 3 for o in range(mask.bit_length()) if mask >> o & 1][: ROUNDS - 1]
    route = {o: (top, o ^ top) for o in wanted}
    if 3 in wanted:
        route[3] = (2, 1) if 5 in wanted or 4 in wanted else (1, 2)
    pairs, labels = [], list(wanted)
    if wanted == [3]:
        pairs = [with_swap(split_hop(here[1], here[2], (2, 1)))]
    elif len(wanted) == 2 and 4 not in wanted:
        (src0, hop0), (src1, hop1) = route[wanted[0]], route[wanted[1]]
        got0 = split_hop(here[src0], here[src1], (hop0, hop1))
        got1 = split_hop(here[src1], here[src0], (hop1, hop0))
        pairs = [(got0, swap(got1)), (got1, swap(got0))]
        labels = [tuple(wanted), tuple(wanted[::-1])]
    else:
        pairs = [with_swap(hop(here[src], by)) for src, by in (route[o] for o in wanted)]
    if not pairs:
        return correlate(plan, turned, [with_swap(crossed)], [top], out)
    out = correlate(plan, turned, [with_swap(crossed)], [top], out)
    return correlate(plan, turned, pairs, labels, out)


def fetch_by_bits(spec, plan):
    bits = lax.axis_size("chan").bit_length() - 1
    partners = [spec] * ROUNDS
    for bit in range(bits):
        moves = jnp.right_shift(plan, bit) & 1 == 1
        for r in range(ROUNDS):
            partners[r] = lax.cond(moves[r], partial(hop, offset=2**bit), lambda v: v, partners[r])
    return partners


def on_device(record, flags, plan):
    windows, width, samples = record.shape
    n_chan = lax.axis_size("chan")
    depth = windows * 2 * NFREQ
    basis, sums = basis_table(samples)
    spec = pl.pallas_call(
        spectra_kernel,
        out_shape=VMEM((depth, width), BF16),
        in_specs=[pl.BlockSpec(memory_space=pl.ANY)] * 4,
        out_specs=pl.BlockSpec(memory_space=VMEM),
        scratch_shapes=[
            pltpu.VMEM((windows, padded(samples), width), BF16),
            pltpu.VMEM(basis.shape, BF16),
            pltpu.VMEM(sums.shape, F32),
            pltpu.VMEM((1, width), jnp.int32),
            pltpu.SemaphoreType.DMA((windows + 3,)),
        ],
        compiler_params=pltpu.CompilerParams(vmem_limit_bytes=66_000_000),
        name="spectra",
    )(flags.reshape(1, width), jnp.asarray(basis), jnp.asarray(sums), record.transpose(0, 2, 1))

    if few_sets(n_chan):
        crossed = hop(spec, n_chan - 1)
        near = [hop(spec, 1), hop(spec, 2)]
        turned, mask = turn(spec, samples, plan)
        out = correlate(plan, turned, [with_swap(block) for block in near], [1, 2])
        branches = [partial(correlate_rest, m) for m in range(2 ** (n_chan - 4))]
        return lax.switch(mask[0], branches, crossed, near, turned, plan, out)
    pairs = [with_swap(m) for m in fetch_by_bits(spec, plan)]
    return correlate(plan, turn(spec, samples, plan)[0], pairs, [None] * ROUNDS)


def solution(mesh):
    def step(record, flags, plan):
        return on_device(record, flags, plan)

    step = jax.shard_map(
        step,
        mesh=mesh,
        in_specs=(P("tm", ("groups", "chan"), None), P(("groups", "chan")), P()),
        out_specs=P("tm", None, ("groups", "chan"), None),
        check_vma=False,
    )
    return step
```

profile of v0, /device:TPU:0, one launch (start us, length us, event | category | flops | bytes accessed | tf_op | source)
XLA Modules:
  0.0 28.9 jit_solution(13567877376787561795)
XLA Ops:
  0.0 3.1 %spectra.1.mine_ref = bf16[256,256]{1,0:T(8,128)(2,1)S(1)} custom-call(s32[1,256]{1,0:T(1,128)} %bitcast.4, bf16[80,1024]{1,0:T(8,128)(2,1)} %constant.30.clone.basis_hbm, f32[64,128]{1,0:T(8,128)} %constant.31.clone.sums_hbm, bf16[4,1000,256]{2,1,0:T(8,128)(2,1)} %bitcast.3), custom_call_target="tpu_custom_call" | custom-call | tf_op jit(solution)/shard_map/spectra/pallas_call | solution.py:254
  3.1 3.1 %collective-permute-start.81 = (bf16[256,256]{1,0:T(8,128)(2,1)S(1)}, bf16[256,256]{1,0:T(8,128)(2,1)S(1)}, u32[]{:S(2)}, u32[]{:S(2)}) collective-permute-start(bf16[256,256]{1,0:T(8,128)(2,1)S(1)} %spectra.1.mine_ref), channel_id=1, source_target_pairs={{0,4},{2,6},{4,0},{6,2},{8,12},{10,14},{12,8},{14,10},{1,5},{3,7},... | collective-permute-start | bytes 393224 | tf_op jit(solution)/shard_map/ppermute | solution.py:197
  6.2 1.5 %collective-permute-start.80 = (bf16[256,256]{1,0:T(8,128)(2,1)S(1)}, bf16[256,256]{1,0:T(8,128)(2,1)S(1)}, u32[]{:S(2)}, u32[]{:S(2)}) collective-permute-start(bf16[256,256]{1,0:T(8,128)(2,1)S(1)} %spectra.1.mine_ref), channel_id=1, source_target_pairs={{0,2},{2,0},{4,6},{6,4},{8,10},{10,8},{12,14},{14,12},{1,3},{3,1},... | collective-permute-start | bytes 393224 | tf_op jit(solution)/shard_map/ppermute | solution.py:197
  7.7 0.0 collective-permute-start.78
  7.7 2.0 %collective-permute-done.81.refs_1_ = bf16[256,256]{1,0:T(8,128)(2,1)S(1)} collective-permute-done((bf16[256,256]{1,0:T(8,128)(2,1)S(1)}, bf16[256,256]{1,0:T(8,128)(2,1)S(1)}, u32[]{:S(2)}, u32[]{:S(2)}) %collective-permute-start.81) | collective-permute-done | bytes 131104 | tf_op jit(solution)/shard_map/ppermute | solution.py:197
  9.7 0.0 collective-permute-start.83
  9.7 1.5 %collective-permute-done.80.refs_0_ = bf16[256,256]{1,0:T(8,128)(2,1)S(1)} collective-permute-done((bf16[256,256]{1,0:T(8,128)(2,1)S(1)}, bf16[256,256]{1,0:T(8,128)(2,1)S(1)}, u32[]{:S(2)}, u32[]{:S(2)}) %collective-permute-start.80) | collective-permute-done | bytes 131104 | tf_op jit(solution)/shard_map/ppermute | solution.py:197
  11.2 0.0 collective-permute-start.82
  11.2 3.7 %collective-permute-start.79 = (bf16[256,256]{1,0:T(8,128)(2,1)S(1)}, bf16[256,256]{1,0:T(8,128)(2,1)S(1)}, u32[]{:S(2)}, u32[]{:S(2)}) collective-permute-start(bf16[256,256]{1,0:T(8,128)(2,1)S(1)} %spectra.1.mine_ref), channel_id=1, source_target_pairs={{0,14},{2,12},{4,10},{6,8},{8,6},{10,4},{12,2},{14,0},{1,15},{3,13... | collective-permute-start | bytes 393224 | tf_op jit(solution)/shard_map/ppermute | solution.py:197
  14.9 0.0 collective-permute-done.78.other_ref
  14.9 1.2 %turn.1 = (bf16[2,256,512]{2,1,0:T(8,128)(2,1)S(1)}, s32[1]{0:T(128)}) custom-call(s32[4]{0:T(128)S(1)} %copy-done.1, bf16[256,256]{1,0:T(8,128)(2,1)S(1)} %spectra.1.mine_ref, bf16[256,256]{1,0:T(8,128)(2,1)S(1)} %collective-permute-done.78.other_ref, f32[4,2,32,128]{3,2,1,0:T(8,128)S(1)} %copy-done), custom_call_target="tpu_custom_call" | custom-call | flops 4194304 | bytes 4194304 | tf_op jit(solution)/shard_map/turn/pallas_call | solution.py:174
  16.8 0.0 collective-permute-done.83.refs_3_
  16.9 0.0 collective-permute-done.82.refs_2_
  16.9 1.9 %correlate.63 = bf16[2,4,256,256]{3,2,1,0:T(8,128)(2,1)} custom-call(s32[4]{0:T(128)S(1)} %copy-done.1, bf16[2,256,512]{2,1,0:T(8,128)(2,1)S(1)} %get-tuple-element.244.turned_ref, bf16[256,256]{1,0:T(8,128)(2,1)S(1)} %collective-permute-done.80.refs_0_, bf16[256,256]{1,0:T(8,128)(2,1)S(1)} %collective-permute-done.81.refs_1_, ...), custom_call_target="tpu_custom_call" | custom-call | flops 536870912 | bytes 2097152 | tf_op jit(solution)/shard_map/correlate/pallas_call | solution.py:155
  18.8 1.1 %collective-permute-done.79 = bf16[256,256]{1,0:T(8,128)(2,1)S(1)} collective-permute-done((bf16[256,256]{1,0:T(8,128)(2,1)S(1)}, bf16[256,256]{1,0:T(8,128)(2,1)S(1)}, u32[]{:S(2)}, u32[]{:S(2)}) %collective-permute-start.79) | collective-permute-done | bytes 131104 | tf_op jit(solution)/shard_map/ppermute | solution.py:197
  19.9 8.8 %conditional.1 = (bf16[2,4,256,256]{3,2,1,0:T(8,128)(2,1)}) conditional(s32[]{:T(128)} %bitcast.2, (bf16[256,256]{1,0:T(8,128)(2,1)S(1)}, s32[4]{0:T(128)S(1)}, bf16[2,256,512]{2,1,0:T(8,128)(2,1)S(1)}, bf16[2,4,256,256]{3,2,1,0:T(8,128)(2,1)}) %tuple.91, (bf16[256,256]{1,0:T(8,128)(2,1)S(1)}, ...), branch_computations={%region_0.0_spmd, %region_1.2_spmd, %region_2.3_spmd, %region_3.4_... | conditional | flops 1073741824 | bytes 7864608 | solution.py:276
  19.9 2.4 %collective-permute-start.65 = (bf16[256,256]{1,0:T(8,128)(2,1)S(1)}, bf16[256,256]{1,0:T(8,128)(2,1)S(1)}, u32[]{:S(2)}, u32[]{:S(2)}) collective-permute-start(bf16[256,256]{1,0:T(8,128)(2,1)S(1)} %broadcast_select_fusion), channel_id=1, source_target_pairs={{0,4},{1,3},{2,6},{3,1},{4,0},{5,7},{6,2},{7,5},{8,12},{9,11},{10,... | collective-permute-start | bytes 393224 | tf_op jit(solution)/shard_map/cond/branch_1_fun/ppermute | solution.py:212
  22.3 0.0 collective-permute-start.67
  22.3 2.9 %collective-permute-done.65.refs_0_ = bf16[256,256]{1,0:T(8,128)(2,1)S(1)} collective-permute-done((bf16[256,256]{1,0:T(8,128)(2,1)S(1)}, bf16[256,256]{1,0:T(8,128)(2,1)S(1)}, u32[]{:S(2)}, u32[]{:S(2)}) %collective-permute-start.65) | collective-permute-done | bytes 131104 | tf_op jit(solution)/shard_map/cond/branch_1_fun/ppermute | solution.py:212
  25.3 0.0 collective-permute-start.66
  25.3 0.0 collective-permute-done.67.refs_1_
  25.3 1.6 %correlate.33.refs_2_ = bf16[2,4,256,256]{3,2,1,0:T(8,128)(2,1)} custom-call(s32[4]{0:T(128)S(1)} %get-tuple-element.159.plan_ref, bf16[2,256,512]{2,1,0:T(8,128)(2,1)S(1)} %get-tuple-element.160.turned_ref, bf16[256,256]{1,0:T(8,128)(2,1)S(1)} %get-tuple-element.168.refs_0_, ...), custom_call_target="tpu_custom_call", output_to_operand_aliasing={{}: (4, {})} | custom-call | flops 268435456 | bytes 1048576 | tf_op jit(solution)/shard_map/cond/branch_1_fun/correlate/pallas_call | solution.py:155
  26.9 0.0 collective-permute-done.66.refs_1_
  26.9 1.6 %correlate.34 = bf16[2,4,256,256]{3,2,1,0:T(8,128)(2,1)} custom-call(s32[4]{0:T(128)S(1)} %get-tuple-element.159.plan_ref, bf16[2,256,512]{2,1,0:T(8,128)(2,1)S(1)} %get-tuple-element.160.turned_ref, bf16[256,256]{1,0:T(8,128)(2,1)S(1)} %collective-permute-done.65.refs_0_, ...), custom_call_target="tpu_custom_call", output_to_operand_aliasing={{}: (4, {})} | custom-call | flops 268435456 | bytes 1048576 | tf_op jit(solution)/shard_map/cond/branch_1_fun/correlate/pallas_call | solution.py:155
  (5 shorter events, 0.0 us)
Async XLA Ops:
  0.0 14.9 %copy-start = (f32[4,2,32,128]{3,2,1,0:T(8,128)S(1)}, f32[4,2,32,128]{3,2,1,0:T(8,128)}, u32[]{:S(2)}) copy-start(f32[4,2,32,128]{3,2,1,0:T(8,128)} %constant.32.clone.table_ref) | copy-start | bytes 393220
  0.0 14.9 %copy-start.1 = (s32[4]{0:T(128)S(1)}, s32[4]{0:T(128)}, u32[]{:S(2)}) copy-start(s32[4]{0:T(128)} %plan_ref.3) | copy-start | bytes 52
  3.1 6.6 %collective-permute-start.81 = (bf16[256,256]{1,0:T(8,128)(2,1)S(1)}, bf16[256,256]{1,0:T(8,128)(2,1)S(1)}, u32[]{:S(2)}, u32[]{:S(2)}) collective-permute-start(bf16[256,256]{1,0:T(8,128)(2,1)S(1)} %spectra.1.mine_ref), channel_id=1, source_target_pairs={{0,4},{2,6},{4,0},{6,2},{8,12},{10,14},{12,8},{14,10},{1,5},{3,7},... | collective-permute-start | bytes 393224 | tf_op jit(solution)/shard_map/ppermute | solution.py:197
  6.2 5.0 %collective-permute-start.80 = (bf16[256,256]{1,0:T(8,128)(2,1)S(1)}, bf16[256,256]{1,0:T(8,128)(2,1)S(1)}, u32[]{:S(2)}, u32[]{:S(2)}) collective-permute-start(bf16[256,256]{1,0:T(8,128)(2,1)S(1)} %spectra.1.mine_ref), channel_id=1, source_target_pairs={{0,2},{2,0},{4,6},{6,4},{8,10},{10,8},{12,14},{14,12},{1,3},{3,1},... | collective-permute-start | bytes 393224 | tf_op jit(solution)/shard_map/ppermute | solution.py:197
  7.7 7.2 %collective-permute-start.78 = (bf16[256,256]{1,0:T(8,128)(2,1)S(1)}, bf16[256,256]{1,0:T(8,128)(2,1)S(1)}, u32[]{:S(2)}, u32[]{:S(2)}) collective-permute-start(bf16[256,256]{1,0:T(8,128)(2,1)S(1)} %spectra.1.mine_ref), channel_id=1, source_target_pairs={{0,1},{1,0},{2,3},{3,2},{4,5},{5,4},{6,7},{7,6},{8,9},{9,8},{10,11... | collective-permute-start | bytes 393224 | tf_op jit(solution)/shard_map/ppermute | solution.py:201
  9.7 7.1 %collective-permute-start.83 = (bf16[256,256]{1,0:T(8,128)(2,1)S(1)}, bf16[256,256]{1,0:T(8,128)(2,1)S(1)}, u32[]{:S(2)}, u32[]{:S(2)}) collective-permute-start(bf16[256,256]{1,0:T(8,128)(2,1)S(1)} %collective-permute-done.81.refs_1_), channel_id=1, source_target_pairs={{0,1},{1,0},{2,3},{3,2},{4,5},{5,4},{6,7},{7,6},{8,9},{9,8},{10,11... | collective-permute-start | bytes 393224 | tf_op jit(solution)/shard_map/ppermute | solution.py:201
  11.2 5.7 %collective-permute-start.82 = (bf16[256,256]{1,0:T(8,128)(2,1)S(1)}, bf16[256,256]{1,0:T(8,128)(2,1)S(1)}, u32[]{:S(2)}, u32[]{:S(2)}) collective-permute-start(bf16[256,256]{1,0:T(8,128)(2,1)S(1)} %collective-permute-done.80.refs_0_), channel_id=1, source_target_pairs={{0,1},{1,0},{2,3},{3,2},{4,5},{5,4},{6,7},{7,6},{8,9},{9,8},{10,11... | collective-permute-start | bytes 393224 | tf_op jit(solution)/shard_map/ppermute | solution.py:201
  11.2 8.7 %collective-permute-start.79 = (bf16[256,256]{1,0:T(8,128)(2,1)S(1)}, bf16[256,256]{1,0:T(8,128)(2,1)S(1)}, u32[]{:S(2)}, u32[]{:S(2)}) collective-permute-start(bf16[256,256]{1,0:T(8,128)(2,1)S(1)} %spectra.1.mine_ref), channel_id=1, source_target_pairs={{0,14},{2,12},{4,10},{6,8},{8,6},{10,4},{12,2},{14,0},{1,15},{3,13... | collective-permute-start | bytes 393224 | tf_op jit(solution)/shard_map/ppermute | solution.py:197
  19.9 5.4 %collective-permute-start.65 = (bf16[256,256]{1,0:T(8,128)(2,1)S(1)}, bf16[256,256]{1,0:T(8,128)(2,1)S(1)}, u32[]{:S(2)}, u32[]{:S(2)}) collective-permute-start(bf16[256,256]{1,0:T(8,128)(2,1)S(1)} %broadcast_select_fusion), channel_id=1, source_target_pairs={{0,4},{1,3},{2,6},{3,1},{4,0},{5,7},{6,2},{7,5},{8,12},{9,11},{10,... | collective-permute-start | bytes 393224 | tf_op jit(solution)/shard_map/cond/branch_1_fun/ppermute | solution.py:212
  22.3 3.0 %collective-permute-start.67 = (bf16[256,256]{1,0:T(8,128)(2,1)S(1)}, bf16[256,256]{1,0:T(8,128)(2,1)S(1)}, u32[]{:S(2)}, u32[]{:S(2)}) collective-permute-start(bf16[256,256]{1,0:T(8,128)(2,1)S(1)} %get-tuple-element.168.refs_0_), channel_id=1, source_target_pairs={{0,1},{1,0},{2,3},{3,2},{4,5},{5,4},{6,7},{7,6},{8,9},{9,8},{10,11... | collective-permute-start | bytes 393224 | tf_op jit(solution)/shard_map/cond/branch_1_fun/ppermute | solution.py:201
  25.3 1.6 %collective-permute-start.66 = (bf16[256,256]{1,0:T(8,128)(2,1)S(1)}, bf16[256,256]{1,0:T(8,128)(2,1)S(1)}, u32[]{:S(2)}, u32[]{:S(2)}) collective-permute-start(bf16[256,256]{1,0:T(8,128)(2,1)S(1)} %collective-permute-done.65.refs_0_), channel_id=1, source_target_pairs={{0,1},{1,0},{2,3},{3,2},{4,5},{5,4},{6,7},{7,6},{8,9},{9,8},{10,11... | collective-permute-start | bytes 393224 | tf_op jit(solution)/shard_map/cond/branch_1_fun/ppermute | solution.py:201
where the time goes:
time: 29 us; the launch traced here: 28.9 us
  starting transfers between devices  10.8 us (37%)
  Pallas kernels  9.37 us (32%)
  waiting for transfers between devices  7.57 us (26%)
  between operations  0.88 us (3%)
    ppermute x3, starting transfers between devices, hop(): return lax.ppermute(value, 'chan', pairs)  8.34 us
    pallas_call x3, Pallas kernels, correlate(): pl.pallas_call(partial(correlate_kernel, scale, labels), out_shape=HBM((l...  5.03 us
    ppermute x3, waiting for transfers between devices, hop(): return lax.ppermute(value, 'chan', pairs)  4.61 us
    pallas_call x1, Pallas kernels, on_device(): pl.pallas_call(spectra_kernel, out_shape=VMEM((depth, width), BF16), in_s...  3.09 us
    ppermute x1, waiting for transfers between devices, split_hop(): return lax.ppermute(value, ('chan', 'tm'), pairs)  2.94 us
    ppermute x1, starting transfers between devices, split_hop(): return lax.ppermute(value, ('chan', 'tm'), pairs)  2.41 us
    pallas_call x1, Pallas kernels, turn(): pl.pallas_call(partial(turn_kernel, lax.axis_size('chan')), out_shape=(ja...  1.24 us
  transfers between devices with their start and end apart: 9, of which 4 were waited for; matrix products, arithmetic and copies ran while one was open for 0% of the time, Pallas kernels for 16%

commit v1 on v0

--- a/solution.py
+++ b/solution.py
@@ -46,14 +46,6 @@
     angle = phase.astype(np.float32) * np.float32(TWO_PI / samples)
     table = np.stack([np.cos(angle), np.sin(angle)], 1).astype(np.float32)
     return np.repeat(table[..., None], 128, 3)
-
-
-def rest_mask(n_chan, plan):
-    mask = jnp.int32(0)
-    for o in range(3, n_chan - 1):
-        for r in range(ROUNDS):
-            mask += (plan[r] == o).astype(jnp.int32) << (o - 3)
-    return mask
 
 
 def place_of(offset, plan):
@@ -91,8 +83,7 @@
         spec_ref[w * rows : (w + 1) * rows, :] = ((out[:rows] - sums * mean) * scale).astype(BF16)
 
 
-def turn_kernel(n_chan, plan_ref, mine_ref, other_ref, table_ref, turned_ref, mask_ref):
-    mask_ref[0] = rest_mask(n_chan, [plan_ref[r] for r in range(ROUNDS)]) if few_sets(n_chan) else jnp.int32(0)
+def turn_kernel(mine_ref, other_ref, table_ref, turned_ref):
     lags = turned_ref.shape[0]
     first = lax.axis_index("tm") * lags
     depth, width = mine_ref.shape
@@ -168,21 +159,17 @@
     )(*given)
 
 
-def turn(spec, samples, plan):
+def turn(spec, other, samples):
     depth, width = spec.shape
-    other = swap(spec)
     return pl.pallas_call(
-        partial(turn_kernel, lax.axis_size("chan")),
-        out_shape=(
-            jax.ShapeDtypeStruct((LAGS // 2, width, 2 * depth), BF16),
-            jax.ShapeDtypeStruct((1,), jnp.int32),
-        ),
-        in_specs=[pl.BlockSpec(memory_space=SMEM)] + [pl.BlockSpec(memory_space=VMEM)] * 3,
-        out_specs=(pl.BlockSpec(memory_space=VMEM), pl.BlockSpec(memory_space=SMEM)),
+        turn_kernel,
+        out_shape=VMEM((LAGS // 2, width, 2 * depth), BF16),
+        in_specs=[pl.BlockSpec(memory_space=VMEM)] * 3,
+        out_specs=pl.BlockSpec(memory_space=VMEM),
         compiler_params=pltpu.CompilerParams(vmem_limit_bytes=KERNEL_VMEM),
         cost_estimate=pl.CostEstimate(flops=4 << 20, bytes_accessed=4 << 20, transcendentals=0),
         name="turn",
-    )(plan, spec, other, jnp.asarray(turn_table(samples)))
+    )(spec, other, jnp.asarray(turn_table(samples)))
 
 
 KERNEL_VMEM = 8 << 20
@@ -203,37 +190,6 @@
 
 def with_swap(block):
     return block, swap(block)
-
-
-def split_hop(first, second, hops):
-    n_chan = lax.axis_size("chan")
-    value = first if first is second else jnp.where(lax.axis_index("tm") == 0, first, second)
-    pairs = [(2 * c + t, 2 * (c ^ hops[t]) + t) for c in range(n_chan) for t in range(2)]
-    return lax.ppermute(value, ("chan", "tm"), pairs)
-
-
-def correlate_rest(mask, crossed, near, turned, plan, out):
-    top = lax.axis_size("chan") - 1
-    here = {1: near[0], 2: near[1], top: crossed}
-    wanted = [o + 3 for o in range(mask.bit_length()) if mask >> o & 1][: ROUNDS - 1]
-    route = {o: (top, o ^ top) for o in wanted}
-    if 3 in wanted:
-        route[3] = (2, 1) if 5 in wanted or 4 in wanted else (1, 2)
-    pairs, labels = [], list(wanted)
-    if wanted == [3]:
-        pairs = [with_swap(split_hop(here[1], here[2], (2, 1)))]
-    elif len(wanted) == 2 and 4 not in wanted:
-        (src0, hop0), (src1, hop1) = route[wanted[0]], route[wanted[1]]
-        got0 = split_hop(here[src0], here[src1], (hop0, hop1))
-        got1 = split_hop(here[src1], here[src0], (hop1, hop0))
-        pairs = [(got0, swap(got1)), (got1, swap(got0))]
-        labels = [tuple(wanted), tuple(wanted[::-1])]
-    else:
-        pairs = [with_swap(hop(here[src], by)) for src, by in (route[o] for o in wanted)]
-    if not pairs:
-        return correlate(plan, turned, [with_swap(crossed)], [top], out)
-    out = correlate(plan, turned, [with_swap(crossed)], [top], out)
-    return correlate(plan, turned, pairs, labels, out)
 
 
 def fetch_by_bits(spec, plan):
@@ -267,15 +223,25 @@
         name="spectra",
     )(flags.reshape(1, width), jnp.asarray(basis), jnp.asarray(sums), record.transpose(0, 2, 1))
 
-    if few_sets(n_chan):
-        crossed = hop(spec, n_chan - 1)
-        near = [hop(spec, 1), hop(spec, 2)]
-        turned, mask = turn(spec, samples, plan)
-        out = correlate(plan, turned, [with_swap(block) for block in near], [1, 2])
-        branches = [partial(correlate_rest, m) for m in range(2 ** (n_chan - 4))]
-        return lax.switch(mask[0], branches, crossed, near, turned, plan, out)
-    pairs = [with_swap(m) for m in fetch_by_bits(spec, plan)]
-    return correlate(plan, turn(spec, samples, plan)[0], pairs, [None] * ROUNDS)
+    if not few_sets(n_chan):
+        pairs = [with_swap(m) for m in fetch_by_bits(spec, plan)]
+        return correlate(plan, turn(spec, swap(spec), samples), pairs, [None] * ROUNDS)
+
+    got = {0: spec}
+    for offset, source in HOPS:
+        got[offset] = hop(got[source], offset ^ source)
+    pairs = {}
+    for offset in got:
+        pairs[offset] = with_swap(got[offset])
+    turned = turn(*pairs[0], samples)
+    out = None
+    for group in GROUPS:
+        out = correlate(plan, turned, [pairs[o] for o in group], group, out)
+    return out
+
+
+HOPS = ((7, 0), (2, 0), (1, 0), (6, 0), (5, 7), (4, 2), (3, 2))
+GROUPS = ((7, 2, 1, 6), (5, 4, 3))
 
 
 def solution(mesh):

time: 29 us -> 31.9 us (1.100)
  waiting for transfers between devices: 7.57 us -> 12.4 us
  Pallas kernels: 9.37 us -> 7.22 us
  starting transfers between devices: 10.8 us -> 12.1 us
  between operations: 0.88 us -> 0.09 us
    ppermute x3 -> x7, waiting for transfers between devices: 4.61 us -> 12.4 us  [hop(): return lax.ppermute(value, 'chan', pairs)]
    ppermute x3 -> x7, starting transfers between devices: 8.34 us -> 11.5 us  [hop(): return lax.ppermute(value, 'chan', pairs)]
    ppermute x1 -> x0, waiting for transfers between devices: 2.94 us -> none  [split_hop(): return lax.ppermute(value, ('chan', 'tm'), pairs)]
    ppermute x1 -> x0, starting transfers between devices: 2.41 us -> none  [split_hop(): return lax.ppermute(value, ('chan', 'tm'), pairs)]
    pallas_call x3 -> x2, Pallas kernels: 5.03 us -> 3.87 us  [correlate(): pl.pallas_call(partial(correlate_kernel, scale, labels), out_shape=HBM((l...]
    pallas_call x1, Pallas kernels: 1.24 us -> 0.26 us  [turn(): pl.pallas_call(turn_kernel, out_shape=VMEM((LAGS // 2, width, 2 * depth),...]
    ppermute x5 -> x8, starting transfers between devices: 0.01 us -> 0.59 us  [swap(): return lax.ppermute(value, 'tm', [(0, 1), (1, 0)])]
  transfers between devices with their start and end apart: 9 -> 15, of which waited for: 4 -> 6; matrix products, arithmetic and copies ran while one was open for 0% -> 0% of each run, Pallas kernels for 16% -> 8%
where the time goes in v1:
time: 31.9 us; the launch traced here: 31.8 us
  waiting for transfers between devices  12.4 us (39%)
  starting transfers between devices  12.1 us (38%)
  Pallas kernels  7.22 us (23%)
    ppermute x7, waiting for transfers between devices, hop(): return lax.ppermute(value, 'chan', pairs)  12.4 us
    ppermute x7, starting transfers between devices, hop(): return lax.ppermute(value, 'chan', pairs)  11.5 us
    pallas_call x2, Pallas kernels, correlate(): pl.pallas_call(partial(correlate_kernel, scale, labels), out_shape=HBM((l...  3.87 us
    pallas_call x1, Pallas kernels, on_device(): pl.pallas_call(spectra_kernel, out_shape=VMEM((depth, width), BF16), in_s...  3.09 us
  transfers between devices with their start and end apart: 15, of which 6 were waited for; matrix products, arithmetic and copies ran while one was open for 0% of the time, Pallas kernels for 8%

profile of v1, /device:TPU:0, one launch (start us, length us, event | category | flops | bytes accessed | tf_op | source)
XLA Modules:
  0.0 31.8 jit_solution(3849144324914015403)
XLA Ops:
  0.0 3.1 %spectra.1.mine_ref = bf16[256,256]{1,0:T(8,128)(2,1)S(1)} custom-call(s32[1,256]{1,0:T(1,128)} %bitcast.3, bf16[80,1024]{1,0:T(8,128)(2,1)} %constant.6.clone.basis_hbm, f32[64,128]{1,0:T(8,128)} %constant.7.clone.sums_hbm, bf16[4,1000,256]{2,1,0:T(8,128)(2,1)} %bitcast.2), custom_call_target="tpu_custom_call" | custom-call | tf_op jit(solution)/shard_map/spectra/pallas_call | solution.py:210
  3.1 5.1 %collective-permute-start.10 = (bf16[256,256]{1,0:T(8,128)(2,1)S(1)}, bf16[256,256]{1,0:T(8,128)(2,1)S(1)}, u32[]{:S(2)}, u32[]{:S(2)}) collective-permute-start(bf16[256,256]{1,0:T(8,128)(2,1)S(1)} %spectra.1.mine_ref), channel_id=1, source_target_pairs={{0,12},{2,14},{4,8},{6,10},{8,4},{10,6},{12,0},{14,2},{1,13},{3,15... | collective-permute-start | bytes 393224 | tf_op jit(solution)/shard_map/ppermute | solution.py:184
  8.2 1.5 %collective-permute-start.9 = (bf16[256,256]{1,0:T(8,128)(2,1)S(1)}, bf16[256,256]{1,0:T(8,128)(2,1)S(1)}, u32[]{:S(2)}, u32[]{:S(2)}) collective-permute-start(bf16[256,256]{1,0:T(8,128)(2,1)S(1)} %spectra.1.mine_ref), channel_id=1, source_target_pairs={{0,2},{2,0},{4,6},{6,4},{8,10},{10,8},{12,14},{14,12},{1,3},{3,1},... | collective-permute-start | bytes 393224 | tf_op jit(solution)/shard_map/ppermute | solution.py:184
  9.7 0.0 collective-permute-start.3
  9.7 0.9 %collective-permute-start.1 = (bf16[256,256]{1,0:T(8,128)(2,1)S(1)}, bf16[256,256]{1,0:T(8,128)(2,1)S(1)}, u32[]{:S(2)}, u32[]{:S(2)}) collective-permute-start(bf16[256,256]{1,0:T(8,128)(2,1)S(1)} %spectra.1.mine_ref), channel_id=1, source_target_pairs={{0,14},{2,12},{4,10},{6,8},{8,6},{10,4},{12,2},{14,0},{1,15},{3,13... | collective-permute-start | bytes 393224 | tf_op jit(solution)/shard_map/ppermute | solution.py:184
  10.6 0.0 collective-permute-start
  10.6 2.0 %collective-permute-done.10.refs_3_ = bf16[256,256]{1,0:T(8,128)(2,1)S(1)} collective-permute-done((bf16[256,256]{1,0:T(8,128)(2,1)S(1)}, bf16[256,256]{1,0:T(8,128)(2,1)S(1)}, u32[]{:S(2)}, u32[]{:S(2)}) %collective-permute-start.10) | collective-permute-done | bytes 131104 | tf_op jit(solution)/shard_map/ppermute | solution.py:184
  12.7 0.6 %collective-permute-done.9.refs_2_ = bf16[256,256]{1,0:T(8,128)(2,1)S(1)} collective-permute-done((bf16[256,256]{1,0:T(8,128)(2,1)S(1)}, bf16[256,256]{1,0:T(8,128)(2,1)S(1)}, u32[]{:S(2)}, u32[]{:S(2)}) %collective-permute-start.9) | collective-permute-done | bytes 131104 | tf_op jit(solution)/shard_map/ppermute | solution.py:184
  13.2 4.5 %collective-permute-done.3.refs_1_ = bf16[256,256]{1,0:T(8,128)(2,1)S(1)} collective-permute-done((bf16[256,256]{1,0:T(8,128)(2,1)S(1)}, bf16[256,256]{1,0:T(8,128)(2,1)S(1)}, u32[]{:S(2)}, u32[]{:S(2)}) %collective-permute-start.3) | collective-permute-done | bytes 131104 | tf_op jit(solution)/shard_map/ppermute | solution.py:184
  17.7 0.8 %collective-permute-done.1.refs_0_ = bf16[256,256]{1,0:T(8,128)(2,1)S(1)} collective-permute-done((bf16[256,256]{1,0:T(8,128)(2,1)S(1)}, bf16[256,256]{1,0:T(8,128)(2,1)S(1)}, u32[]{:S(2)}, u32[]{:S(2)}) %collective-permute-start.1) | collective-permute-done | bytes 131104 | tf_op jit(solution)/shard_map/ppermute | solution.py:184
  18.5 3.4 %collective-permute-start.4 = (bf16[256,256]{1,0:T(8,128)(2,1)S(1)}, bf16[256,256]{1,0:T(8,128)(2,1)S(1)}, u32[]{:S(2)}, u32[]{:S(2)}) collective-permute-start(bf16[256,256]{1,0:T(8,128)(2,1)S(1)} %collective-permute-done.3.refs_1_), channel_id=1, source_target_pairs={{0,12},{2,14},{4,8},{6,10},{8,4},{10,6},{12,0},{14,2},{1,13},{3,15... | collective-permute-start | bytes 393224 | tf_op jit(solution)/shard_map/ppermute | solution.py:184
  22.0 0.0 collective-permute-done.other_ref
  22.0 0.5 %collective-permute-start.2 = (bf16[256,256]{1,0:T(8,128)(2,1)S(1)}, bf16[256,256]{1,0:T(8,128)(2,1)S(1)}, u32[]{:S(2)}, u32[]{:S(2)}) collective-permute-start(bf16[256,256]{1,0:T(8,128)(2,1)S(1)} %collective-permute-done.1.refs_0_), channel_id=1, source_target_pairs={{0,4},{2,6},{4,0},{6,2},{8,12},{10,14},{12,8},{14,10},{1,5},{3,7},... | collective-permute-start | bytes 393224 | tf_op jit(solution)/shard_map/ppermute | solution.py:184
  22.5 0.5 %collective-permute-start.11 = (bf16[256,256]{1,0:T(8,128)(2,1)S(1)}, bf16[256,256]{1,0:T(8,128)(2,1)S(1)}, u32[]{:S(2)}, u32[]{:S(2)}) collective-permute-start(bf16[256,256]{1,0:T(8,128)(2,1)S(1)} %collective-permute-done.1.refs_0_), channel_id=1, source_target_pairs={{0,1},{1,0},{2,3},{3,2},{4,5},{5,4},{6,7},{7,6},{8,9},{9,8},{10,11... | collective-permute-start | bytes 393224 | tf_op jit(solution)/shard_map/ppermute | solution.py:188
  23.0 0.1 collective-permute-start.8
  23.1 3.1 %collective-permute-done.4.refs_1_ = bf16[256,256]{1,0:T(8,128)(2,1)S(1)} collective-permute-done((bf16[256,256]{1,0:T(8,128)(2,1)S(1)}, bf16[256,256]{1,0:T(8,128)(2,1)S(1)}, u32[]{:S(2)}, u32[]{:S(2)}) %collective-permute-start.4) | collective-permute-done | bytes 131104 | tf_op jit(solution)/shard_map/ppermute | solution.py:184
  26.2 1.4 %collective-permute-done.2.refs_0_ = bf16[256,256]{1,0:T(8,128)(2,1)S(1)} collective-permute-done((bf16[256,256]{1,0:T(8,128)(2,1)S(1)}, bf16[256,256]{1,0:T(8,128)(2,1)S(1)}, u32[]{:S(2)}, u32[]{:S(2)}) %collective-permute-start.2) | collective-permute-done | bytes 131104 | tf_op jit(solution)/shard_map/ppermute | solution.py:184
  27.5 0.0 collective-permute-start.6
  27.5 0.3 turn.1.turned_ref
  27.8 0.0 collective-permute-done.12.refs_5_
  27.8 2.3 %correlate.2.refs_6_ = bf16[2,4,256,256]{3,2,1,0:T(8,128)(2,1)} custom-call(s32[4]{0:T(128)S(1)} %copy-done.1, bf16[2,256,512]{2,1,0:T(8,128)(2,1)S(1)} %turn.1.turned_ref, bf16[256,256]{1,0:T(8,128)(2,1)S(1)} %collective-permute-done.1.refs_0_, bf16[256,256]{1,0:T(8,128)(2,1)S(1)} %collective-permute-done.3.refs_1_, ...), custom_call_target="tpu_custom_call" | custom-call | flops 1073741824 | bytes 4194304 | tf_op jit(solution)/shard_map/correlate/pallas_call | solution.py:146
  30.1 0.0 collective-permute-done.8.refs_5_
  30.1 0.0 collective-permute-done.6.refs_3_
  30.1 1.6 %correlate.3 = bf16[2,4,256,256]{3,2,1,0:T(8,128)(2,1)} custom-call(s32[4]{0:T(128)S(1)} %copy-done.1, bf16[2,256,512]{2,1,0:T(8,128)(2,1)S(1)} %turn.1.turned_ref, bf16[256,256]{1,0:T(8,128)(2,1)S(1)} %collective-permute-done.2.refs_0_, bf16[256,256]{1,0:T(8,128)(2,1)S(1)} %collective-permute-done.4.refs_1_, ...), custom_call_target="tpu_custom_call", output_to_operand_aliasing={{}: (8, {})} | custom-call | flops 805306368 | bytes 3145728 | tf_op jit(solution)/shard_map/correlate/pallas_call | solution.py:146
  (14 shorter events, 0.0 us)
Async XLA Ops:
  0.0 27.5 %copy-start = (f32[4,2,32,128]{3,2,1,0:T(8,128)S(1)}, f32[4,2,32,128]{3,2,1,0:T(8,128)}, u32[]{:S(2)}) copy-start(f32[4,2,32,128]{3,2,1,0:T(8,128)} %constant.8.clone.table_ref) | copy-start | bytes 393220
  0.0 27.8 %copy-start.1 = (s32[4]{0:T(128)S(1)}, s32[4]{0:T(128)}, u32[]{:S(2)}) copy-start(s32[4]{0:T(128)} %plan_ref.3) | copy-start | bytes 52
  3.1 9.5 %collective-permute-start.10 = (bf16[256,256]{1,0:T(8,128)(2,1)S(1)}, bf16[256,256]{1,0:T(8,128)(2,1)S(1)}, u32[]{:S(2)}, u32[]{:S(2)}) collective-permute-start(bf16[256,256]{1,0:T(8,128)(2,1)S(1)} %spectra.1.mine_ref), channel_id=1, source_target_pairs={{0,12},{2,14},{4,8},{6,10},{8,4},{10,6},{12,0},{14,2},{1,13},{3,15... | collective-permute-start | bytes 393224 | tf_op jit(solution)/shard_map/ppermute | solution.py:184
  8.2 5.0 %collective-permute-start.9 = (bf16[256,256]{1,0:T(8,128)(2,1)S(1)}, bf16[256,256]{1,0:T(8,128)(2,1)S(1)}, u32[]{:S(2)}, u32[]{:S(2)}) collective-permute-start(bf16[256,256]{1,0:T(8,128)(2,1)S(1)} %spectra.1.mine_ref), channel_id=1, source_target_pairs={{0,2},{2,0},{4,6},{6,4},{8,10},{10,8},{12,14},{14,12},{1,3},{3,1},... | collective-permute-start | bytes 393224 | tf_op jit(solution)/shard_map/ppermute | solution.py:184
  9.7 8.0 %collective-permute-start.3 = (bf16[256,256]{1,0:T(8,128)(2,1)S(1)}, bf16[256,256]{1,0:T(8,128)(2,1)S(1)}, u32[]{:S(2)}, u32[]{:S(2)}) collective-permute-start(bf16[256,256]{1,0:T(8,128)(2,1)S(1)} %spectra.1.mine_ref), channel_id=1, source_target_pairs={{0,4},{2,6},{4,0},{6,2},{8,12},{10,14},{12,8},{14,10},{1,5},{3,7},... | collective-permute-start | bytes 393224 | tf_op jit(solution)/shard_map/ppermute | solution.py:184
  9.7 8.8 %collective-permute-start.1 = (bf16[256,256]{1,0:T(8,128)(2,1)S(1)}, bf16[256,256]{1,0:T(8,128)(2,1)S(1)}, u32[]{:S(2)}, u32[]{:S(2)}) collective-permute-start(bf16[256,256]{1,0:T(8,128)(2,1)S(1)} %spectra.1.mine_ref), channel_id=1, source_target_pairs={{0,14},{2,12},{4,10},{6,8},{8,6},{10,4},{12,2},{14,0},{1,15},{3,13... | collective-permute-start | bytes 393224 | tf_op jit(solution)/shard_map/ppermute | solution.py:184
  10.6 11.4 %collective-permute-start = (bf16[256,256]{1,0:T(8,128)(2,1)S(1)}, bf16[256,256]{1,0:T(8,128)(2,1)S(1)}, u32[]{:S(2)}, u32[]{:S(2)}) collective-permute-start(bf16[256,256]{1,0:T(8,128)(2,1)S(1)} %spectra.1.mine_ref), channel_id=1, source_target_pairs={{0,1},{1,0},{2,3},{3,2},{4,5},{5,4},{6,7},{7,6},{8,9},{9,8},{10,11... | collective-permute-start | bytes 393224 | tf_op jit(solution)/shard_map/ppermute | solution.py:188
  12.6 9.8 %collective-permute-start.14 = (bf16[256,256]{1,0:T(8,128)(2,1)S(1)}, bf16[256,256]{1,0:T(8,128)(2,1)S(1)}, u32[]{:S(2)}, u32[]{:S(2)}) collective-permute-start(bf16[256,256]{1,0:T(8,128)(2,1)S(1)} %collective-permute-done.10.refs_3_), channel_id=1, source_target_pairs={{0,1},{1,0},{2,3},{3,2},{4,5},{5,4},{6,7},{7,6},{8,9},{9,8},{10,11... | collective-permute-start | bytes 393224 | tf_op jit(solution)/shard_map/ppermute | solution.py:188
  13.2 9.3 %collective-permute-start.13 = (bf16[256,256]{1,0:T(8,128)(2,1)S(1)}, bf16[256,256]{1,0:T(8,128)(2,1)S(1)}, u32[]{:S(2)}, u32[]{:S(2)}) collective-permute-start(bf16[256,256]{1,0:T(8,128)(2,1)S(1)} %collective-permute-done.9.refs_2_), channel_id=1, source_target_pairs={{0,1},{1,0},{2,3},{3,2},{4,5},{5,4},{6,7},{7,6},{8,9},{9,8},{10,11... | collective-permute-start | bytes 393224 | tf_op jit(solution)/shard_map/ppermute | solution.py:188
  17.7 5.3 %collective-permute-start.5 = (bf16[256,256]{1,0:T(8,128)(2,1)S(1)}, bf16[256,256]{1,0:T(8,128)(2,1)S(1)}, u32[]{:S(2)}, u32[]{:S(2)}) collective-permute-start(bf16[256,256]{1,0:T(8,128)(2,1)S(1)} %collective-permute-done.3.refs_1_), channel_id=1, source_target_pairs={{0,2},{2,0},{4,6},{6,4},{8,10},{10,8},{12,14},{14,12},{1,3},{3,1},... | collective-permute-start | bytes 393224 | tf_op jit(solution)/shard_map/ppermute | solution.py:184
  18.5 7.6 %collective-permute-start.4 = (bf16[256,256]{1,0:T(8,128)(2,1)S(1)}, bf16[256,256]{1,0:T(8,128)(2,1)S(1)}, u32[]{:S(2)}, u32[]{:S(2)}) collective-permute-start(bf16[256,256]{1,0:T(8,128)(2,1)S(1)} %collective-permute-done.3.refs_1_), channel_id=1, source_target_pairs={{0,12},{2,14},{4,8},{6,10},{8,4},{10,6},{12,0},{14,2},{1,13},{3,15... | collective-permute-start | bytes 393224 | tf_op jit(solution)/shard_map/ppermute | solution.py:184
  22.0 5.6 %collective-permute-start.2 = (bf16[256,256]{1,0:T(8,128)(2,1)S(1)}, bf16[256,256]{1,0:T(8,128)(2,1)S(1)}, u32[]{:S(2)}, u32[]{:S(2)}) collective-permute-start(bf16[256,256]{1,0:T(8,128)(2,1)S(1)} %collective-permute-done.1.refs_0_), channel_id=1, source_target_pairs={{0,4},{2,6},{4,0},{6,2},{8,12},{10,14},{12,8},{14,10},{1,5},{3,7},... | collective-permute-start | bytes 393224 | tf_op jit(solution)/shard_map/ppermute | solution.py:184
  22.5 5.3 %collective-permute-start.12 = (bf16[256,256]{1,0:T(8,128)(2,1)S(1)}, bf16[256,256]{1,0:T(8,128)(2,1)S(1)}, u32[]{:S(2)}, u32[]{:S(2)}) collective-permute-start(bf16[256,256]{1,0:T(8,128)(2,1)S(1)} %collective-permute-done.3.refs_1_), channel_id=1, source_target_pairs={{0,1},{1,0},{2,3},{3,2},{4,5},{5,4},{6,7},{7,6},{8,9},{9,8},{10,11... | collective-permute-start | bytes 393224 | tf_op jit(solution)/shard_map/ppermute | solution.py:188
  22.5 5.3 %collective-permute-start.11 = (bf16[256,256]{1,0:T(8,128)(2,1)S(1)}, bf16[256,256]{1,0:T(8,128)(2,1)S(1)}, u32[]{:S(2)}, u32[]{:S(2)}) collective-permute-start(bf16[256,256]{1,0:T(8,128)(2,1)S(1)} %collective-permute-done.1.refs_0_), channel_id=1, source_target_pairs={{0,1},{1,0},{2,3},{3,2},{4,5},{5,4},{6,7},{7,6},{8,9},{9,8},{10,11... | collective-permute-start | bytes 393224 | tf_op jit(solution)/shard_map/ppermute | solution.py:188
  23.0 7.1 %collective-permute-start.8 = (bf16[256,256]{1,0:T(8,128)(2,1)S(1)}, bf16[256,256]{1,0:T(8,128)(2,1)S(1)}, u32[]{:S(2)}, u32[]{:S(2)}) collective-permute-start(bf16[256,256]{1,0:T(8,128)(2,1)S(1)} %collective-permute-done.5.refs_2_), channel_id=1, source_target_pairs={{0,1},{1,0},{2,3},{3,2},{4,5},{5,4},{6,7},{7,6},{8,9},{9,8},{10,11... | collective-permute-start | bytes 393224 | tf_op jit(solution)/shard_map/ppermute | solution.py:188
  26.2 4.0 %collective-permute-start.7 = (bf16[256,256]{1,0:T(8,128)(2,1)S(1)}, bf16[256,256]{1,0:T(8,128)(2,1)S(1)}, u32[]{:S(2)}, u32[]{:S(2)}) collective-permute-start(bf16[256,256]{1,0:T(8,128)(2,1)S(1)} %collective-permute-done.4.refs_1_), channel_id=1, source_target_pairs={{0,1},{1,0},{2,3},{3,2},{4,5},{5,4},{6,7},{7,6},{8,9},{9,8},{10,11... | collective-permute-start | bytes 393224 | tf_op jit(solution)/shard_map/ppermute | solution.py:188
  27.5 2.6 %collective-permute-start.6 = (bf16[256,256]{1,0:T(8,128)(2,1)S(1)}, bf16[256,256]{1,0:T(8,128)(2,1)S(1)}, u32[]{:S(2)}, u32[]{:S(2)}) collective-permute-start(bf16[256,256]{1,0:T(8,128)(2,1)S(1)} %collective-permute-done.2.refs_0_), channel_id=1, source_target_pairs={{0,1},{1,0},{2,3},{3,2},{4,5},{5,4},{6,7},{7,6},{8,9},{9,8},{10,11... | collective-permute-start | bytes 393224 | tf_op jit(solution)/shard_map/ppermute | solution.py:188

commit v2 on v1

--- a/solution.py
+++ b/solution.py
@@ -1,4 +1,5 @@
 from functools import partial
+import itertools
 import math
 
 import numpy as np
@@ -48,14 +49,32 @@
     return np.repeat(table[..., None], 128, 3)
 
 
+def offset_sets(n_chan):
+    return sorted(itertools.combinations(range(1, n_chan - 1), ROUNDS - 1), key=lambda s: s[::-1])
+
+
+def set_index(plan):
+    index = jnp.int32(0)
+    for r in range(ROUNDS):
+        rank = sum((plan[j] < plan[r]).astype(jnp.int32) for j in range(ROUNDS) if j != r)
+        below = plan[r] - 1
+        pairs = below * (below - 1) // 2
+        triples = below * (below - 1) * (below - 2) // 6
+        term = jnp.where(rank == 0, below, jnp.where(rank == 1, pairs, triples))
+        index += jnp.where(rank == ROUNDS - 1, 0, term)
+    return index
+
+
 def place_of(offset, plan):
-    place = jnp.int32(ROUNDS)
+    place = jnp.int32(0)
     for r in range(ROUNDS):
         place = jnp.where(plan[r] == offset, r, place)
     return place
 
 
-def spectra_kernel(flags_hbm, basis_hbm, sums_hbm, record_hbm, spec_ref, held, basis, sums_held, flags, sems):
+def spectra_kernel(
+    n_chan, plan_ref, flags_hbm, basis_hbm, sums_hbm, record_hbm, spec_ref, index_ref, held, basis, sums_held, flags, sems
+):
     windows, samples, width = record_hbm.shape
     copies = [
         pltpu.make_async_copy(record_hbm.at[w], held.at[w, pl.ds(0, samples)], sems.at[w]) for w in range(windows)
@@ -65,6 +84,7 @@
     copies[0].start()
     for copy in small + copies[1:]:
         copy.start()
+    index_ref[0] = set_index([plan_ref[r] for r in range(ROUNDS)]) if few_sets(n_chan) else jnp.int32(0)
     pad = held.shape[1] - samples
     for w in range(windows):
         held[w, samples:, :] = jnp.zeros((pad, width), BF16)
@@ -87,10 +107,12 @@
     lags = turned_ref.shape[0]
     first = lax.axis_index("tm") * lags
     depth, width = mine_ref.shape
-    for half, ref in enumerate((mine_ref, other_ref)):
-        for lag in range(lags):
-            cosine = jnp.concatenate([table_ref[first + lag, 0]] * (width // 128), axis=1)
-            sine = jnp.concatenate([table_ref[first + lag, 1]] * (width // 128), axis=1)
+
+    @pl.loop(0, lags)
+    def _(lag):
+        cosine = jnp.concatenate([table_ref[first + lag, 0]] * (width // 128), axis=1)
+        sine = jnp.concatenate([table_ref[first + lag, 1]] * (width // 128), axis=1)
+        for half, ref in enumerate((mine_ref, other_ref)):
             parts = []
             for w in range(depth // (2 * NFREQ)):
                 start = w * 2 * NFREQ
@@ -111,27 +133,22 @@
     for s, label in enumerate(labels):
         if isinstance(label, tuple):
             label = jnp.where(lax.axis_index("tm") == 0, *label)
-        places.append(jnp.int32(s) if label is None else place_of(label, plan))
+        places.append(s if label is None else place_of(label, plan))
 
     def copy(s, lag):
         return pltpu.make_async_copy(held.at[s, lag], out_ref.at[lag, places[s]], sems.at[s, lag])
 
+    @pl.loop(0, lags)
+    def _(lag):
+        for s in range(blocks):
+            total = jnp.dot(turned_ref[lag, :, :half], mine[s][...], preferred_element_type=F32)
+            total += jnp.dot(turned_ref[lag, :, half:], other[s][...], preferred_element_type=F32)
+            held[s, lag] = (total * scale).astype(BF16)
+            copy(s, lag).start()
+
     for s in range(blocks):
-
-        @pl.when(places[s] < ROUNDS)
-        def _():
-            for lag in range(lags):
-                total = jnp.dot(turned_ref[lag, :, :half], mine[s][...], preferred_element_type=F32)
-                total += jnp.dot(turned_ref[lag, :, half:], other[s][...], preferred_element_type=F32)
-                held[s, lag] = (total * scale).astype(BF16)
-                copy(s, lag).start()
-
-    for s in range(blocks):
-
-        @pl.when(places[s] < ROUNDS)
-        def _():
-            for lag in range(lags):
-                copy(s, lag).wait()
+        for lag in range(lags):
+            copy(s, lag).wait()
 
 
 def correlate(plan, turned, pairs, labels, out=None):
@@ -159,7 +176,7 @@
     )(*given)
 
 
-def turn(spec, other, samples):
+def turn(spec, other, table):
     depth, width = spec.shape
     return pl.pallas_call(
         turn_kernel,
@@ -169,7 +186,7 @@
         compiler_params=pltpu.CompilerParams(vmem_limit_bytes=KERNEL_VMEM),
         cost_estimate=pl.CostEstimate(flops=4 << 20, bytes_accessed=4 << 20, transcendentals=0),
         name="turn",
-    )(spec, other, jnp.asarray(turn_table(samples)))
+    )(spec, other, table)
 
 
 KERNEL_VMEM = 8 << 20
@@ -207,11 +224,11 @@
     n_chan = lax.axis_size("chan")
     depth = windows * 2 * NFREQ
     basis, sums = basis_table(samples)
-    spec = pl.pallas_call(
-        spectra_kernel,
-        out_shape=VMEM((depth, width), BF16),
-        in_specs=[pl.BlockSpec(memory_space=pl.ANY)] * 4,
-        out_specs=pl.BlockSpec(memory_space=VMEM),
+    spec, index = pl.pallas_call(
+        partial(spectra_kernel, n_chan),
+        out_shape=(VMEM((depth, width), BF16), jax.ShapeDtypeStruct((1,), jnp.int32)),
+        in_specs=[pl.BlockSpec(memory_space=SMEM)] + [pl.BlockSpec(memory_space=pl.ANY)] * 4,
+        out_specs=(pl.BlockSpec(memory_space=VMEM), pl.BlockSpec(memory_space=SMEM)),
         scratch_shapes=[
             pltpu.VMEM((windows, padded(samples), width), BF16),
             pltpu.VMEM(basis.shape, BF16),
@@ -221,38 +238,66 @@
         ],
         compiler_params=pltpu.CompilerParams(vmem_limit_bytes=66_000_000),
         name="spectra",
-    )(flags.reshape(1, width), jnp.asarray(basis), jnp.asarray(sums), record.transpose(0, 2, 1))
-
+    )(plan, flags.reshape(1, width), jnp.asarray(basis), jnp.asarray(sums), record.transpose(0, 2, 1))
+
+    table = lax.optimization_barrier(jnp.asarray(turn_table(samples)))
     if not few_sets(n_chan):
         pairs = [with_swap(m) for m in fetch_by_bits(spec, plan)]
-        return correlate(plan, turn(spec, swap(spec), samples), pairs, [None] * ROUNDS)
-
+        return correlate(plan, turn(spec, swap(spec), table), pairs, [None] * ROUNDS)
+    branches = [partial(correlate_set, route_of(o)) for o in offset_sets(n_chan)]
+    return lax.switch(index[0], branches, spec, plan, table)
+
+
+def route_of(offsets):
+    wanted = sorted(offsets) + [7]
+    far = [o for o in wanted if o >= 4]
+    near = [o for o in wanted if o < 4]
+    cross = max(far, key=lambda c: (sum(o ^ c in (1, 2) for o in far), -c))
+    first, later = [cross], [(o, cross) for o in far if o ^ cross == 3]
+    beside = [o for o in far if o ^ cross in (1, 2)]
+    later += [(tuple(beside), cross)] if len(beside) == 2 else [(o, cross) for o in beside]
+    if near == [1, 2, 3]:
+        near, later = [1, 2], later + [(3, 2)]
+    return first + near, later
+
+
+def split_hops(value, hops):
+    n_chan = lax.axis_size("chan")
+    pairs = [(2 * c + t, 2 * (c ^ hops[t]) + t) for c in range(n_chan) for t in range(2)]
+    return lax.ppermute(value, ("chan", "tm"), pairs)
+
+
+def correlate_set(route, spec, plan, table):
+    first, later = route
     got = {0: spec}
-    for offset, source in HOPS:
-        got[offset] = hop(got[source], offset ^ source)
-    pairs = {}
-    for offset in got:
-        pairs[offset] = with_swap(got[offset])
-    turned = turn(*pairs[0], samples)
-    out = None
-    for group in GROUPS:
-        out = correlate(plan, turned, [pairs[o] for o in group], group, out)
-    return out
-
-
-HOPS = ((7, 0), (2, 0), (1, 0), (6, 0), (5, 7), (4, 2), (3, 2))
-GROUPS = ((7, 2, 1, 6), (5, 4, 3))
+
+    def swapped(offset):
+        return swap(got[offset])
+
+    for offset in first:
+        got[offset] = hop(spec, offset)
+    last, labels = [], []
+    for offset, source in later:
+        if isinstance(offset, tuple):
+            low, high = offset
+            for a, b in ((low, high), (high, low)):
+                got[a] = split_hops(got[source], (a ^ source, b ^ source))
+            last += [(got[low], swapped(high)), (got[high], swapped(low))]
+            labels += [(low, high), (high, low)]
+        else:
+            got[offset] = hop(got[source], offset ^ source)
+            last.append((got[offset], swapped(offset)))
+            labels.append(offset)
+    turned = turn(spec, swapped(0), table)
+    out = correlate(plan, turned, [(got[o], swapped(o)) for o in first], first)
+    return correlate(plan, turned, last, labels, out)
 
 
 def solution(mesh):
-    def step(record, flags, plan):
-        return on_device(record, flags, plan)
-
-    step = jax.shard_map(
-        step,
+    return jax.shard_map(
+        on_device,
         mesh=mesh,
         in_specs=(P("tm", ("groups", "chan"), None), P(("groups", "chan")), P()),
         out_specs=P("tm", None, ("groups", "chan"), None),
         check_vma=False,
     )
-    return step

time: 31.9 us -> 23.9 us (0.75)
  waiting for transfers between devices: 12.4 us -> 4.71 us
  starting transfers between devices: 12.1 us -> 9.57 us
  between operations: 0.09 us -> 0.9 us
  Pallas kernels: 7.22 us -> 7.93 us
  loops' own time: 0 us -> 0.63 us
    ppermute x7 -> x4, waiting for transfers between devices: 12.4 us -> 4.69 us  [hop(): return lax.ppermute(value, 'chan', pairs)]
    ppermute x7 -> x4, starting transfers between devices: 11.5 us -> 8.54 us  [hop(): return lax.ppermute(value, 'chan', pairs)]
    pallas_call x1, Pallas kernels: 3.09 us -> 3.89 us  [on_device(): pl.pallas_call(partial(spectra_kernel, n_chan), out_shape=(VMEM((depth, w...]
    another operation x0 -> x1, loops' own time: none -> 0.63 us  [on_device(): return lax.switch(index[0], branches, spec, plan, table)]
    ppermute x8 -> x5, starting transfers between devices: 0.59 us -> 1.02 us  [swap(): return lax.ppermute(value, 'tm', [(0, 1), (1, 0)])]
  transfers between devices with their start and end apart: 15 -> 9, of which waited for: 6 -> 2; matrix products, arithmetic and copies ran while one was open for 0% -> 0% of each run, Pallas kernels for 8% -> 10%
where the time goes in v2:
time: 23.9 us; the launch traced here: 23.7 us
  starting transfers between devices  9.57 us (40%)
  Pallas kernels  7.93 us (33%)
  waiting for transfers between devices  4.71 us (20%)
  between operations  0.9 us (4%)
  loops' own time  0.63 us (3%)
    ppermute x4, starting transfers between devices, hop(): return lax.ppermute(value, 'chan', pairs)  8.54 us
    ppermute x4, waiting for transfers between devices, hop(): return lax.ppermute(value, 'chan', pairs)  4.69 us
    pallas_call x1, Pallas kernels, on_device(): pl.pallas_call(partial(spectra_kernel, n_chan), out_shape=(VMEM((depth, w...  3.89 us
    pallas_call x2, Pallas kernels, correlate(): pl.pallas_call(partial(correlate_kernel, scale, labels), out_shape=HBM((l...  3.74 us
    ppermute x5, starting transfers between devices, swap(): return lax.ppermute(value, 'tm', [(0, 1), (1, 0)])  1.02 us
    another operation x1, loops' own time, on_device(): return lax.switch(index[0], branches, spec, plan, table)  0.63 us
  transfers between devices with their start and end apart: 9, of which 2 were waited for; matrix products, arithmetic and copies ran while one was open for 0% of the time, Pallas kernels for 10%

profile of v2, /device:TPU:0, one launch (start us, length us, event | category | flops | bytes accessed | tf_op | source)
XLA Modules:
  0.0 23.7 jit_solution(14551468777008750553)
XLA Ops:
  0.0 3.9 %spectra.1 = (bf16[256,256]{1,0:T(8,128)(2,1)S(1)}, s32[1]{0:T(128)}) custom-call(s32[4]{0:T(128)} %plan_ref.1, s32[1,256]{1,0:T(1,128)} %bitcast.4, bf16[80,1024]{1,0:T(8,128)(2,1)} %constant.12.clone.basis_hbm, f32[64,128]{1,0:T(8,128)} %constant.13.clone.sums_hbm, bf16[4,1000,256]{2,1,0:T(8,128)(2,1)} %bitcast.3), custom_call_target="tpu_custom_call" | custom-call | tf_op jit(solution)/shard_map/spectra/pallas_call | solution.py:227
  4.6 0.0 copy-done
  4.6 19.0 %conditional.1 = (bf16[2,4,256,256]{3,2,1,0:T(8,128)(2,1)}) conditional(s32[]{:T(128)} %bitcast.2, (bf16[256,256]{1,0:T(8,128)(2,1)S(1)}, f32[4,2,32,128]{3,2,1,0:T(8,128)S(1)}, s32[4]{0:T(128)S(1)}) %tuple.126, (bf16[256,256]{1,0:T(8,128)(2,1)S(1)}, f32[4,2,32,128]{3,2,1,0:T(8,128)S(1)}, s32[4]{0:T(128)S(1)}) %tuple.127, ...), branch_computations={%region_0.0_spmd, %region_1.0_spmd, %region_2.0_spmd, %region_3.0_... | conditional | flops 1077936128 | bytes 13107568 | solution.py:248
  4.6 3.1 %collective-permute-start.1 = (bf16[256,256]{1,0:T(8,128)(2,1)S(1)}, bf16[256,256]{1,0:T(8,128)(2,1)S(1)}, u32[]{:S(2)}, u32[]{:S(2)}) collective-permute-start(bf16[256,256]{1,0:T(8,128)(2,1)S(1)} %get-tuple-element.129.mine_ref), channel_id=1, source_target_pairs={{0,4},{2,6},{4,0},{6,2},{8,12},{10,14},{12,8},{14,10},{1,5},{3,7},... | collective-permute-start | bytes 393224 | tf_op jit(solution)/shard_map/cond/branch_0_fun/ppermute | solution.py:201
  7.7 1.5 %collective-permute-start.5 = (bf16[256,256]{1,0:T(8,128)(2,1)S(1)}, bf16[256,256]{1,0:T(8,128)(2,1)S(1)}, u32[]{:S(2)}, u32[]{:S(2)}) collective-permute-start(bf16[256,256]{1,0:T(8,128)(2,1)S(1)} %get-tuple-element.129.mine_ref), channel_id=1, source_target_pairs={{0,2},{2,0},{4,6},{6,4},{8,10},{10,8},{12,14},{14,12},{1,3},{3,1},... | collective-permute-start | bytes 393224 | tf_op jit(solution)/shard_map/cond/branch_0_fun/ppermute | solution.py:201
  9.2 2.4 %collective-permute-start.4 = (bf16[256,256]{1,0:T(8,128)(2,1)S(1)}, bf16[256,256]{1,0:T(8,128)(2,1)S(1)}, u32[]{:S(2)}, u32[]{:S(2)}) collective-permute-start(bf16[256,256]{1,0:T(8,128)(2,1)S(1)} %get-tuple-element.129.mine_ref), channel_id=1, source_target_pairs={{0,14},{2,12},{4,10},{6,8},{8,6},{10,4},{12,2},{14,0},{1,15},{3,13... | collective-permute-start | bytes 393224 | tf_op jit(solution)/shard_map/cond/branch_0_fun/ppermute | solution.py:201
  11.7 0.0 collective-permute-done.1.refs_2_
  11.7 1.5 %collective-permute-start.2 = (bf16[256,256]{1,0:T(8,128)(2,1)S(1)}, bf16[256,256]{1,0:T(8,128)(2,1)S(1)}, u32[]{:S(2)}, u32[]{:S(2)}) collective-permute-start(bf16[256,256]{1,0:T(8,128)(2,1)S(1)} %collective-permute-done.1.refs_2_), channel_id=1, source_target_pairs={{0,2},{2,0},{4,6},{6,4},{8,10},{10,8},{12,14},{14,12},{1,3},{3,1},... | collective-permute-start | bytes 393224 | tf_op jit(solution)/shard_map/cond/branch_0_fun/ppermute | solution.py:201
  13.1 0.0 collective-permute-start
  13.2 0.0 collective-permute-done.5.refs_1_
  13.2 0.5 %collective-permute-start.7 = (bf16[256,256]{1,0:T(8,128)(2,1)S(1)}, bf16[256,256]{1,0:T(8,128)(2,1)S(1)}, u32[]{:S(2)}, u32[]{:S(2)}) collective-permute-start(bf16[256,256]{1,0:T(8,128)(2,1)S(1)} %collective-permute-done.5.refs_1_), channel_id=1, source_target_pairs={{0,1},{1,0},{2,3},{3,2},{4,5},{5,4},{6,7},{7,6},{8,9},{9,8},{10,11... | collective-permute-start | bytes 393224 | tf_op jit(solution)/shard_map/cond/branch_0_fun/ppermute | solution.py:205
  13.7 3.6 %collective-permute-done.4.refs_0_ = bf16[256,256]{1,0:T(8,128)(2,1)S(1)} collective-permute-done((bf16[256,256]{1,0:T(8,128)(2,1)S(1)}, bf16[256,256]{1,0:T(8,128)(2,1)S(1)}, u32[]{:S(2)}, u32[]{:S(2)}) %collective-permute-start.4) | collective-permute-done | bytes 131104 | tf_op jit(solution)/shard_map/cond/branch_0_fun/ppermute | solution.py:201
  17.2 0.0 collective-permute-start.6
  17.2 0.5 %collective-permute-start.8 = (bf16[256,256]{1,0:T(8,128)(2,1)S(1)}, bf16[256,256]{1,0:T(8,128)(2,1)S(1)}, u32[]{:S(2)}, u32[]{:S(2)}) collective-permute-start(bf16[256,256]{1,0:T(8,128)(2,1)S(1)} %collective-permute-done.1.refs_2_), channel_id=1, source_target_pairs={{0,1},{1,0},{2,3},{3,2},{4,5},{5,4},{6,7},{7,6},{8,9},{9,8},{10,11... | collective-permute-start | bytes 393224 | tf_op jit(solution)/shard_map/cond/branch_0_fun/ppermute | solution.py:205
  17.8 1.1 %collective-permute-done.2.refs_0_ = bf16[256,256]{1,0:T(8,128)(2,1)S(1)} collective-permute-done((bf16[256,256]{1,0:T(8,128)(2,1)S(1)}, bf16[256,256]{1,0:T(8,128)(2,1)S(1)}, u32[]{:S(2)}, u32[]{:S(2)}) %collective-permute-start.2) | collective-permute-done | bytes 131104 | tf_op jit(solution)/shard_map/cond/branch_0_fun/ppermute | solution.py:201
  18.9 0.0 collective-permute-start.3
  18.9 0.0 collective-permute-done.other_ref
  18.9 0.3 %turn.20.turned_ref = bf16[2,256,512]{2,1,0:T(8,128)(2,1)S(1)} custom-call(bf16[256,256]{1,0:T(8,128)(2,1)S(1)} %get-tuple-element.129.mine_ref, bf16[256,256]{1,0:T(8,128)(2,1)S(1)} %collective-permute-done.other_ref, f32[4,2,32,128]{3,2,1,0:T(8,128)S(1)} %get-tuple-element.130.table_ref), custom_call_target="tpu_custom_call" | custom-call | flops 4194304 | bytes 4194304 | tf_op jit(solution)/shard_map/cond/branch_0_fun/turn/pallas_call | solution.py:181
  19.2 0.0 collective-permute-done.7.refs_4_
  19.2 0.0 collective-permute-done.6.refs_3_
  19.2 0.0 collective-permute-done.8.refs_5_
  19.2 2.1 %correlate.40.refs_2_ = bf16[2,4,256,256]{3,2,1,0:T(8,128)(2,1)} custom-call(s32[4]{0:T(128)S(1)} %get-tuple-element.128.plan_ref, bf16[2,256,512]{2,1,0:T(8,128)(2,1)S(1)} %turn.20.turned_ref, bf16[256,256]{1,0:T(8,128)(2,1)S(1)} %collective-permute-done.4.refs_0_, bf16[256,256]{1,0:T(8,128)(2,1)S(1)} %collective-permute-done.5.refs_1_, ...), custom_call_target="tpu_custom_call" | custom-call | flops 805306368 | bytes 3145728 | tf_op jit(solution)/shard_map/cond/branch_0_fun/correlate/pallas_call | solution.py:163
  21.3 0.0 collective-permute-done.3.refs_1_
  21.3 1.7 %correlate.41 = bf16[2,4,256,256]{3,2,1,0:T(8,128)(2,1)} custom-call(s32[4]{0:T(128)S(1)} %get-tuple-element.128.plan_ref, bf16[2,256,512]{2,1,0:T(8,128)(2,1)S(1)} %turn.20.turned_ref, bf16[256,256]{1,0:T(8,128)(2,1)S(1)} %collective-permute-done.2.refs_0_, bf16[256,256]{1,0:T(8,128)(2,1)S(1)} %collective-permute-done.3.refs_1_, ...), custom_call_target="tpu_custom_call", output_to_operand_aliasing={{}: (4, {})} | custom-call | flops 268435456 | bytes 1048576 | tf_op jit(solution)/shard_map/cond/branch_0_fun/correlate/pallas_call | solution.py:163
  (3 shorter events, 0.0 us)
Async XLA Ops:
  0.0 4.6 %copy-start = (f32[4,2,32,128]{3,2,1,0:T(8,128)S(1)}, f32[4,2,32,128]{3,2,1,0:T(8,128)}, u32[]{:S(2)}) copy-start(f32[4,2,32,128]{3,2,1,0:T(8,128)} %constant.14.clone) | copy-start | bytes 393220
  0.0 4.6 %copy-start.1 = (s32[4]{0:T(128)S(1)}, s32[4]{0:T(128)}, u32[]{:S(2)}) copy-start(s32[4]{0:T(128)} %plan_ref.1) | copy-start | bytes 52
  4.6 7.1 %collective-permute-start.1 = (bf16[256,256]{1,0:T(8,128)(2,1)S(1)}, bf16[256,256]{1,0:T(8,128)(2,1)S(1)}, u32[]{:S(2)}, u32[]{:S(2)}) collective-permute-start(bf16[256,256]{1,0:T(8,128)(2,1)S(1)} %get-tuple-element.129.mine_ref), channel_id=1, source_target_pairs={{0,4},{2,6},{4,0},{6,2},{8,12},{10,14},{12,8},{14,10},{1,5},{3,7},... | collective-permute-start | bytes 393224 | tf_op jit(solution)/shard_map/cond/branch_0_fun/ppermute | solution.py:201
  7.7 5.4 %collective-permute-start.5 = (bf16[256,256]{1,0:T(8,128)(2,1)S(1)}, bf16[256,256]{1,0:T(8,128)(2,1)S(1)}, u32[]{:S(2)}, u32[]{:S(2)}) collective-permute-start(bf16[256,256]{1,0:T(8,128)(2,1)S(1)} %get-tuple-element.129.mine_ref), channel_id=1, source_target_pairs={{0,2},{2,0},{4,6},{6,4},{8,10},{10,8},{12,14},{14,12},{1,3},{3,1},... | collective-permute-start | bytes 393224 | tf_op jit(solution)/shard_map/cond/branch_0_fun/ppermute | solution.py:201
  9.2 8.0 %collective-permute-start.4 = (bf16[256,256]{1,0:T(8,128)(2,1)S(1)}, bf16[256,256]{1,0:T(8,128)(2,1)S(1)}, u32[]{:S(2)}, u32[]{:S(2)}) collective-permute-start(bf16[256,256]{1,0:T(8,128)(2,1)S(1)} %get-tuple-element.129.mine_ref), channel_id=1, source_target_pairs={{0,14},{2,12},{4,10},{6,8},{8,6},{10,4},{12,2},{14,0},{1,15},{3,13... | collective-permute-start | bytes 393224 | tf_op jit(solution)/shard_map/cond/branch_0_fun/ppermute | solution.py:201
  11.7 7.2 %collective-permute-start.2 = (bf16[256,256]{1,0:T(8,128)(2,1)S(1)}, bf16[256,256]{1,0:T(8,128)(2,1)S(1)}, u32[]{:S(2)}, u32[]{:S(2)}) collective-permute-start(bf16[256,256]{1,0:T(8,128)(2,1)S(1)} %collective-permute-done.1.refs_2_), channel_id=1, source_target_pairs={{0,2},{2,0},{4,6},{6,4},{8,10},{10,8},{12,14},{14,12},{1,3},{3,1},... | collective-permute-start | bytes 393224 | tf_op jit(solution)/shard_map/cond/branch_0_fun/ppermute | solution.py:201
  13.1 5.7 %collective-permute-start = (bf16[256,256]{1,0:T(8,128)(2,1)S(1)}, bf16[256,256]{1,0:T(8,128)(2,1)S(1)}, u32[]{:S(2)}, u32[]{:S(2)}) collective-permute-start(bf16[256,256]{1,0:T(8,128)(2,1)S(1)} %get-tuple-element.129.mine_ref), channel_id=1, source_target_pairs={{0,1},{1,0},{2,3},{3,2},{4,5},{5,4},{6,7},{7,6},{8,9},{9,8},{10,11... | collective-permute-start | bytes 393224 | tf_op jit(solution)/shard_map/cond/branch_0_fun/ppermute | solution.py:205
  13.2 6.0 %collective-permute-start.7 = (bf16[256,256]{1,0:T(8,128)(2,1)S(1)}, bf16[256,256]{1,0:T(8,128)(2,1)S(1)}, u32[]{:S(2)}, u32[]{:S(2)}) collective-permute-start(bf16[256,256]{1,0:T(8,128)(2,1)S(1)} %collective-permute-done.5.refs_1_), channel_id=1, source_target_pairs={{0,1},{1,0},{2,3},{3,2},{4,5},{5,4},{6,7},{7,6},{8,9},{9,8},{10,11... | collective-permute-start | bytes 393224 | tf_op jit(solution)/shard_map/cond/branch_0_fun/ppermute | solution.py:205
  17.2 2.0 %collective-permute-start.6 = (bf16[256,256]{1,0:T(8,128)(2,1)S(1)}, bf16[256,256]{1,0:T(8,128)(2,1)S(1)}, u32[]{:S(2)}, u32[]{:S(2)}) collective-permute-start(bf16[256,256]{1,0:T(8,128)(2,1)S(1)} %collective-permute-done.4.refs_0_), channel_id=1, source_target_pairs={{0,1},{1,0},{2,3},{3,2},{4,5},{5,4},{6,7},{7,6},{8,9},{9,8},{10,11... | collective-permute-start | bytes 393224 | tf_op jit(solution)/shard_map/cond/branch_0_fun/ppermute | solution.py:205
  17.2 2.0 %collective-permute-start.8 = (bf16[256,256]{1,0:T(8,128)(2,1)S(1)}, bf16[256,256]{1,0:T(8,128)(2,1)S(1)}, u32[]{:S(2)}, u32[]{:S(2)}) collective-permute-start(bf16[256,256]{1,0:T(8,128)(2,1)S(1)} %collective-permute-done.1.refs_2_), channel_id=1, source_target_pairs={{0,1},{1,0},{2,3},{3,2},{4,5},{5,4},{6,7},{7,6},{8,9},{9,8},{10,11... | collective-permute-start | bytes 393224 | tf_op jit(solution)/shard_map/cond/branch_0_fun/ppermute | solution.py:205
  18.9 2.4 %collective-permute-start.3 = (bf16[256,256]{1,0:T(8,128)(2,1)S(1)}, bf16[256,256]{1,0:T(8,128)(2,1)S(1)}, u32[]{:S(2)}, u32[]{:S(2)}) collective-permute-start(bf16[256,256]{1,0:T(8,128)(2,1)S(1)} %collective-permute-done.2.refs_0_), channel_id=1, source_target_pairs={{0,1},{1,0},{2,3},{3,2},{4,5},{5,4},{6,7},{7,6},{8,9},{9,8},{10,11... | collective-permute-start | bytes 393224 | tf_op jit(solution)/shard_map/cond/branch_0_fun/ppermute | solution.py:205
